TPU v7x, 512 devices: a whole 4x4x16 slice. The times are simulated.
512 devices in a mesh: depth: 32 (over x, y, core), strip: 16 (over z).
Axes of the slice: x: 4, y: 4, z: 16, core: 2. Of those that a mesh axis runs over, the one named last changes fastest.
Arguments:
- density: float32 [128, 256, 2048], P('depth', 'strip'), may hold values from -6 to 6
- materials: int32 [128, 256, 2048], P('depth', 'strip'), may hold values from 0 to 3
- occupancy_flags: int32 [32, 16, 16], P('depth', 'strip'), may hold values from 0 to 1, as said below
- tf_color: float32 [4, 3, 16], replicated, may hold values from 0.1 to 1
- tf_opacity: float32 [4, 16], replicated, may hold values from 0.0005 to 0.05
Outputs:
- image: float32 [4, 256, 2048], P(None, 'strip', 'depth')
Inputs may be any that keep to these rules, and one draw needn't show every extreme that they name: `occupancy_flags`: occupied tiles cluster around one depth slab drawn from the seed; the share of occupied tiles differs strongly between depth slabs.
All inputs are finite; a program needn't handle non-finite values.
Results may differ from a plain program's by a relative error of at most 0.0003.
Values sent between devices are 32-bit elements; how exact they have to be, the bound alone decides.
A program may use at most 64 MiB of HBM per device.

v0:
```python
import jax
import jax.numpy as jnp
from jax import lax
from jax.sharding import PartitionSpec as P

light_x = 1.0 / 3.0
light_y = 2.0 / 3.0
light_z = 2.0 / 3.0
ambient = 0.3
diffuse = 0.7


def with_halo(array, sides, width):
    for axis, dim in sides:
        devices, length = (lax.axis_size(axis), array.shape[dim])
        up = [(i, (i + 1) % devices) for i in range(devices - 1)]
        down = [(j, i) for i, j in up]
        last = lax.slice_in_dim(array, length - width, length, axis=dim)
        first = lax.slice_in_dim(array, 0, width, axis=dim)
        before = lax.ppermute(last, axis, up)
        after = lax.ppermute(first, axis, down)
        array = jnp.concatenate([before, array, after], axis=dim)
    return array


def shade_slice(before, here, after, material_slice, occupied, knot_table):
    sample = here[1:-1, 1:-1]
    grad_z = 0.5 * (after[1:-1, 1:-1] - before[1:-1, 1:-1])
    grad_y = 0.5 * (here[2:, 1:-1] - here[:-2, 1:-1])
    grad_x = 0.5 * (here[1:-1, 2:] - here[1:-1, :-2])
    knot_count = knot_table.shape[1]
    material_count = knot_table.shape[0] // 4
    position = jnp.clip(
        (sample.reshape(-1) + 3.0) * ((knot_count - 1) / 6.0), 0.0, knot_count - 1.0
    )
    knot_grid = jnp.arange(knot_count, dtype=jnp.float32)[:, None]
    tent_weights = jnp.maximum(0.0, 1.0 - jnp.abs(position[None, :] - knot_grid))
    looked = jnp.dot(
        knot_table,
        tent_weights,
        precision=lax.Precision.HIGHEST,
        preferred_element_type=jnp.float32,
    )
    onehot = (
        material_slice.reshape(-1)[None, :] == jnp.arange(material_count, dtype=jnp.int32)[:, None]
    ).astype(jnp.float32)
    colour = jnp.sum(
        looked[: 3 * material_count].reshape(material_count, 3, -1) * onehot[:, None, :], axis=0
    )
    density_rate = jnp.sum(looked[3 * material_count :] * onehot, axis=0) * occupied.reshape(-1)
    facing = (grad_x * light_x + grad_y * light_y + grad_z * light_z).reshape(-1)
    steepness = (grad_x * grad_x + grad_y * grad_y + grad_z * grad_z).reshape(-1)
    lighting = ambient + diffuse * jnp.abs(facing) / jnp.sqrt(1.0 + steepness)
    opacity_step = 1.0 - jnp.exp(-density_rate)
    return (colour * (lighting * opacity_step)[None, :], opacity_step)


def composite_over(nearer, farther):
    return jnp.concatenate(
        [nearer[:3] + nearer[3:] * farther[:3], nearer[3:] * farther[3:]], axis=0
    )


def on_device(density, materials, occupancy_flags, tf_color, tf_opacity):
    slab_depth, row_count, columns = density.shape
    material_count = tf_color.shape[0]
    knot_count = tf_color.shape[2]
    knot_table = jnp.concatenate(
        [tf_color.reshape(material_count * 3, knot_count), tf_opacity], axis=0
    )
    padded = with_halo(density, (("depth", 0), ("strip", 1)), 1)
    padded = jnp.pad(padded, ((0, 0), (0, 0), (1, 1)))
    tile_count = occupancy_flags.shape[2]
    tile_row = jnp.repeat(occupancy_flags[0, 0], columns // tile_count).astype(jnp.float32)
    occupied = jnp.broadcast_to(tile_row[None, :], (row_count, columns))

    def advance(state_carry, slab_index):
        radiance, transmit = state_carry
        before = lax.dynamic_index_in_dim(padded, slab_index, 0, keepdims=False)
        here = lax.dynamic_index_in_dim(padded, slab_index + 1, 0, keepdims=False)
        after = lax.dynamic_index_in_dim(padded, slab_index + 2, 0, keepdims=False)
        material_slice = lax.dynamic_index_in_dim(materials, slab_index, 0, keepdims=False)
        emitted, opacity_step = shade_slice(
            before, here, after, material_slice, occupied, knot_table
        )
        return ((radiance + transmit[None, :] * emitted, transmit * (1.0 - opacity_step)), None)

    start = (
        jnp.zeros((3, row_count * columns), jnp.float32),
        jnp.ones((row_count * columns,), jnp.float32),
    )
    (radiance, transmit), _ = lax.scan(advance, start, jnp.arange(slab_depth, dtype=jnp.int32))
    partial_value = jnp.concatenate([radiance, transmit[None, :]], axis=0).reshape(
        4, row_count, columns
    )
    groups = lax.axis_size("depth")
    levels = groups.bit_length() - 1
    block_width = columns // groups
    pieces = lax.all_to_all(partial_value, "depth", split_axis=2, concat_axis=1, tiled=True)
    pieces = pieces.reshape(4, groups, row_count, block_width)
    for section_bit in range(levels):
        pieces = composite_over(pieces[:, 0::2], pieces[:, 1::2])
    finished = pieces[:, 0]
    return jnp.concatenate([finished[:3], 1.0 - finished[3:]], axis=0)


def solution(mesh):
    placed = (
        P("depth", "strip", None),
        P("depth", "strip", None),
        P("depth", "strip", None),
        P(),
        P(),
    )
    return jax.shard_map(
        on_device, mesh=mesh, in_specs=placed, out_specs=P(None, "strip", "depth"), check_vma=False
    )
```

profile of v0, /device:TPU:225, one launch (start us, length us, event | category | flops | bytes accessed | tf_op | source)
XLA Modules:
  0.0 129.5 jit_solution(18345752158085729972)
XLA Ops:
  0.0 1.0 fusion.26
  1.0 2.6 %collective-permute-start.1 = (f32[1,16,2048]{2,1,0:T(8,128)S(1)}, f32[1,16,2048]{2,1,0:T(8,128)S(1)}, u32[]{:S(2)}, u32[]{:S(2)}) collective-permute-start(f32[1,16,2048]{2,1,0:T(8,128)S(1)} %get-tuple-element.198), channel_id=1, source_target_pairs={{16,0},{32,16},{48,32},{64,48},{80,64},{96,80},{112,96},{128,112},... | collective-permute-start | bytes 393224 | tf_op jit(solution)/shard_map/ppermute | solution.py:21
  3.6 3.1 %collective-permute-start = (f32[1,16,2048]{2,1,0:T(8,128)S(1)}, f32[1,16,2048]{2,1,0:T(8,128)S(1)}, u32[]{:S(2)}, u32[]{:S(2)}) collective-permute-start(f32[1,16,2048]{2,1,0:T(8,128)S(1)} %get-tuple-element.199), channel_id=1, source_target_pairs={{0,16},{16,32},{32,48},{48,64},{64,80},{80,96},{96,112},{112,128},... | collective-permute-start | bytes 393224 | tf_op jit(solution)/shard_map/ppermute | solution.py:20
  7.4 0.7 copy.10
  8.6 1.1 constant_dynamic-update-slice_fusion.1
  9.8 4.8 %collective-permute-start.2 = (f32[6,1,2048]{2,1,0:T(1,128)S(1)}, f32[6,1,2048]{2,1,0:T(1,128)S(1)}, u32[]{:S(2)}, u32[]{:S(2)}) collective-permute-start(f32[6,1,2048]{2,1,0:T(1,128)S(1)} %get-tuple-element.194), channel_id=1, source_target_pairs={{0,1},{1,2},{2,3},{3,4},{4,5},{5,6},{6,7},{7,8},{8,9},{9,10},{10,1... | collective-permute-start | bytes 147464 | tf_op jit(solution)/shard_map/ppermute | solution.py:20
  14.6 1.9 %collective-permute-start.3 = (f32[6,1,2048]{2,1,0:T(1,128)S(1)}, f32[6,1,2048]{2,1,0:T(1,128)S(1)}, u32[]{:S(2)}, u32[]{:S(2)}) collective-permute-start(f32[6,1,2048]{2,1,0:T(1,128)S(1)} %get-tuple-element.195), channel_id=1, source_target_pairs={{1,0},{2,1},{3,2},{4,3},{5,4},{6,5},{7,6},{8,7},{9,8},{10,9},{11,1... | collective-permute-start | bytes 147464 | tf_op jit(solution)/shard_map/ppermute | solution.py:21
  16.6 4.2 %collective-permute-done.3 = f32[6,1,2048]{2,1,0:T(1,128)S(1)} collective-permute-done((f32[6,1,2048]{2,1,0:T(1,128)S(1)}, f32[6,1,2048]{2,1,0:T(1,128)S(1)}, u32[]{:S(2)}, u32[]{:S(2)}) %collective-permute-start.3) | collective-permute-done | bytes 49184 | tf_op jit(solution)/shard_map/ppermute | solution.py:21
  21.4 63.1 %while.16 = (s32[]{:T(128)}, f32[3,32768]{1,0:T(4,128)S(1)}, f32[32768]{0:T(1024)}, s32[4]{0:T(128)S(1)}, f32[6,18,2050]{2,1,0:T(8,128)S(1)}, /*index=5*/f32[16,...) while((s32[]{:T(128)}, f32[3,32768]{1,0:T(4,128)S(1)}, ...), condition=%wide.region_3.4_spmd.clone, body=%wide.region_0.3_spmd.clone.sunk | while | flops 105480208 | bytes 23315676 | solution.py:92
  27.1 0.9 dynamic-slice_bitcast_fusion.7
  28.7 2.1 %convolution_bitcast_fusion.2 = f32[16,32768]{1,0:T(8,128)S(1)} fusion(f32[16,16]{1,0:T(8,128)S(1)} %get-tuple-element.308, f32[32768]{0:T(1024)S(1)} %bitcast.78), kind=kOutput, calls=%fused_computation.1.clone.1 | convolution fusion | flops 102760448 | bytes 2229248 | tf_op jit(solution)/shard_map/while/body/eval_jaxpr/dot_general | solution.py:38
  31.3 2.1 %reshape.152 = f32[4,3,32768]{2,1,0:T(4,128)} reshape(f32[12,32768]{1,0:T(8,128)S(1)} %bitcast.70) | data formatting | bytes 3145728 | tf_op jit(solution)/shard_map/while/body/eval_jaxpr/reshape | solution.py:48
  33.4 2.4 %multiply_reduce_fusion.2 = f32[3,32768]{1,0:T(4,128)S(1)} fusion(f32[4,3,32768]{2,1,0:T(4,128)} %reshape.152, f32[4,32768]{1,0:T(4,128)S(1)} %fusion.35), kind=kLoop, calls=%fused_computation.2.clone.1 | loop fusion | flops 688128 | bytes 2490368 | tf_op jit(solution)/shard_map/while/body/eval_jaxpr/reduce_sum | solution.py:47
  42.9 0.9 dynamic-slice_bitcast_fusion.7
  44.5 2.1 %convolution_bitcast_fusion.2 = f32[16,32768]{1,0:T(8,128)S(1)} fusion(f32[16,16]{1,0:T(8,128)S(1)} %get-tuple-element.308, f32[32768]{0:T(1024)S(1)} %bitcast.78), kind=kOutput, calls=%fused_computation.1.clone.1 | convolution fusion | flops 102760448 | bytes 2229248 | tf_op jit(solution)/shard_map/while/body/eval_jaxpr/dot_general | solution.py:38
  47.1 2.1 %reshape.152 = f32[4,3,32768]{2,1,0:T(4,128)} reshape(f32[12,32768]{1,0:T(8,128)S(1)} %bitcast.70) | data formatting | bytes 3145728 | tf_op jit(solution)/shard_map/while/body/eval_jaxpr/reshape | solution.py:48
  49.1 2.4 %multiply_reduce_fusion.2 = f32[3,32768]{1,0:T(4,128)S(1)} fusion(f32[4,3,32768]{2,1,0:T(4,128)} %reshape.152, f32[4,32768]{1,0:T(4,128)S(1)} %fusion.35), kind=kLoop, calls=%fused_computation.2.clone.1 | loop fusion | flops 688128 | bytes 2490368 | tf_op jit(solution)/shard_map/while/body/eval_jaxpr/reduce_sum | solution.py:47
  58.7 0.9 dynamic-slice_bitcast_fusion.7
  60.2 2.1 %convolution_bitcast_fusion.2 = f32[16,32768]{1,0:T(8,128)S(1)} fusion(f32[16,16]{1,0:T(8,128)S(1)} %get-tuple-element.308, f32[32768]{0:T(1024)S(1)} %bitcast.78), kind=kOutput, calls=%fused_computation.1.clone.1 | convolution fusion | flops 102760448 | bytes 2229248 | tf_op jit(solution)/shard_map/while/body/eval_jaxpr/dot_general | solution.py:38
  62.8 2.1 %reshape.152 = f32[4,3,32768]{2,1,0:T(4,128)} reshape(f32[12,32768]{1,0:T(8,128)S(1)} %bitcast.70) | data formatting | bytes 3145728 | tf_op jit(solution)/shard_map/while/body/eval_jaxpr/reshape | solution.py:48
  64.9 2.4 %multiply_reduce_fusion.2 = f32[3,32768]{1,0:T(4,128)S(1)} fusion(f32[4,3,32768]{2,1,0:T(4,128)} %reshape.152, f32[4,32768]{1,0:T(4,128)S(1)} %fusion.35), kind=kLoop, calls=%fused_computation.2.clone.1 | loop fusion | flops 688128 | bytes 2490368 | tf_op jit(solution)/shard_map/while/body/eval_jaxpr/reduce_sum | solution.py:47
  74.4 0.9 dynamic-slice_bitcast_fusion.7
  76.0 2.1 %convolution_bitcast_fusion.2 = f32[16,32768]{1,0:T(8,128)S(1)} fusion(f32[16,16]{1,0:T(8,128)S(1)} %get-tuple-element.308, f32[32768]{0:T(1024)S(1)} %bitcast.78), kind=kOutput, calls=%fused_computation.1.clone.1 | convolution fusion | flops 102760448 | bytes 2229248 | tf_op jit(solution)/shard_map/while/body/eval_jaxpr/dot_general | solution.py:38
  78.6 2.1 %reshape.152 = f32[4,3,32768]{2,1,0:T(4,128)} reshape(f32[12,32768]{1,0:T(8,128)S(1)} %bitcast.70) | data formatting | bytes 3145728 | tf_op jit(solution)/shard_map/while/body/eval_jaxpr/reshape | solution.py:48
  80.6 2.4 %multiply_reduce_fusion.2 = f32[3,32768]{1,0:T(4,128)S(1)} fusion(f32[4,3,32768]{2,1,0:T(4,128)} %reshape.152, f32[4,32768]{1,0:T(4,128)S(1)} %fusion.35), kind=kLoop, calls=%fused_computation.2.clone.1 | loop fusion | flops 688128 | bytes 2490368 | tf_op jit(solution)/shard_map/while/body/eval_jaxpr/reduce_sum | solution.py:47
  84.4 0.9 concatenate.35
  85.7 3.1 %copy.11 = f32[4,16,2048]{1,0,2:T(4,128)} copy(f32[4,16,2048]{2,1,0:T(8,128)S(1)} %pad_maximum_fusion) | data formatting | bytes 1048576 | tf_op jit(solution)/shard_map/concatenate | solution.py:93
  88.7 4.8 %reshape.149 = f32[32,1,4096]{2,1,0:T(1,128)S(1)} reshape(f32[2048,4,16]{2,1,0:T(4,128)} %bitcast.75) | data formatting | bytes 1048576
  93.5 23.0 %all_to_all.15 = f32[32,1,4096]{2,1,0:T(1,128)S(1)} all-to-all(f32[32,1,4096]{2,1,0:T(1,128)S(1)} %reshape.149), channel_id=1, replica_groups=mesh['depth'=32,'strip'=16] {'depth'}, dimensions={0} | all-to-all | bytes 1048576 | tf_op jit(solution)/shard_map/all_to_all | solution.py:99
  117.0 1.9 %reduce = f32[32,4096]{1,0:T(8,128)S(1)} reduce(f32[32,1,4096]{2,1,0:T(1,128)S(1)} %all_to_all.15, f32[]{:T(128)} %broadcast.229), dimensions={1}, to_apply=%all_to_all.11.reduce_sub_computation | reduce | bytes 1048580 | tf_op jit(solution)/shard_map/all_to_all | solution.py:99
  118.9 4.3 %reshape.150 = f32[2048,4,16]{2,1,0:T(4,128)} reshape(f32[32,4096]{1,0:T(8,128)S(1)} %reduce) | data formatting | bytes 1048576
  123.2 3.5 %copy.13 = f32[4,16,32,64]{3,2,1,0:T(8,128)S(1)} copy(f32[4,16,32,64]{1,0,3,2:T(4,128)} %bitcast.74) | data formatting | bytes 1048576 | tf_op jit(solution)/shard_map/all_to_all | solution.py:99
  (137 shorter events, 17.4 us)
Async XLA Ops:
  0.0 16.5 %copy-start.4 = (f32[4,16]{1,0:T(4,128)S(1)}, f32[4,16]{1,0:T(4,128)}, u32[]{:S(2)}) copy-start(f32[4,16]{1,0:T(4,128)} %param.11) | copy-start | bytes 772
  1.0 8.7 %collective-permute-start.1 = (f32[1,16,2048]{2,1,0:T(8,128)S(1)}, f32[1,16,2048]{2,1,0:T(8,128)S(1)}, u32[]{:S(2)}, u32[]{:S(2)}) collective-permute-start(f32[1,16,2048]{2,1,0:T(8,128)S(1)} %get-tuple-element.198), channel_id=1, source_target_pairs={{16,0},{32,16},{48,32},{64,48},{80,64},{96,80},{112,96},{128,112},... | collective-permute-start | bytes 393224 | tf_op jit(solution)/shard_map/ppermute | solution.py:21
  3.6 5.0 %collective-permute-start = (f32[1,16,2048]{2,1,0:T(8,128)S(1)}, f32[1,16,2048]{2,1,0:T(8,128)S(1)}, u32[]{:S(2)}, u32[]{:S(2)}) collective-permute-start(f32[1,16,2048]{2,1,0:T(8,128)S(1)} %get-tuple-element.199), channel_id=1, source_target_pairs={{0,16},{16,32},{32,48},{48,64},{64,80},{80,96},{96,112},{112,128},... | collective-permute-start | bytes 393224 | tf_op jit(solution)/shard_map/ppermute | solution.py:20
  9.8 6.7 %collective-permute-start.2 = (f32[6,1,2048]{2,1,0:T(1,128)S(1)}, f32[6,1,2048]{2,1,0:T(1,128)S(1)}, u32[]{:S(2)}, u32[]{:S(2)}) collective-permute-start(f32[6,1,2048]{2,1,0:T(1,128)S(1)} %get-tuple-element.194), channel_id=1, source_target_pairs={{0,1},{1,2},{2,3},{3,4},{4,5},{5,6},{6,7},{7,8},{8,9},{9,10},{10,1... | collective-permute-start | bytes 147464 | tf_op jit(solution)/shard_map/ppermute | solution.py:20
  14.6 6.1 %collective-permute-start.3 = (f32[6,1,2048]{2,1,0:T(1,128)S(1)}, f32[6,1,2048]{2,1,0:T(1,128)S(1)}, u32[]{:S(2)}, u32[]{:S(2)}) collective-permute-start(f32[6,1,2048]{2,1,0:T(1,128)S(1)} %get-tuple-element.195), channel_id=1, source_target_pairs={{1,0},{2,1},{3,2},{4,3},{5,4},{6,5},{7,6},{8,7},{9,8},{10,9},{11,1... | collective-permute-start | bytes 147464 | tf_op jit(solution)/shard_map/ppermute | solution.py:21
  21.4 6.8 %copy-start.5 = (s32[4]{0:T(128)}, s32[4]{0:T(128)S(1)}, u32[]{:S(2)}) copy-start(s32[4]{0:T(128)S(1)} %get-tuple-element.306) | copy-start | bytes 52 | tf_op jit(solution)/shard_map/while
  21.4 7.3 %copy-start = (f32[6,18,2050]{2,1,0:T(8,128)}, f32[6,18,2050]{2,1,0:T(8,128)S(1)}, u32[]{:S(2)}) copy-start(f32[6,18,2050]{2,1,0:T(8,128)S(1)} %get-tuple-element.307) | copy-start | bytes 2656804 | tf_op jit(solution)/shard_map/while
  33.4 2.5 %copy-start.2 = (f32[32768]{0:T(1024)S(1)}, f32[32768]{0:T(1024)}, u32[]{:S(2)}) copy-start(f32[32768]{0:T(1024)} %get-tuple-element.290) | copy-start | bytes 393220 | tf_op jit(solution)/shard_map/while
  35.8 1.3 %copy-start.1 = (f32[6,18,2050]{2,1,0:T(8,128)S(1)}, f32[6,18,2050]{2,1,0:T(8,128)}, u32[]{:S(2)}) copy-start(f32[6,18,2050]{2,1,0:T(8,128)} %copy-done) | copy-start | bytes 2656804 | tf_op jit(solution)/shard_map/while
  35.8 1.3 %copy-start.6 = (s32[4]{0:T(128)S(1)}, s32[4]{0:T(128)}, u32[]{:S(2)}) copy-start(s32[4]{0:T(128)} %copy-done.5) | copy-start | bytes 52 | tf_op jit(solution)/shard_map/while
  35.9 0.7 copy-start.3
  37.2 6.7 %copy-start.5 = (s32[4]{0:T(128)}, s32[4]{0:T(128)S(1)}, u32[]{:S(2)}) copy-start(s32[4]{0:T(128)S(1)} %get-tuple-element.306) | copy-start | bytes 52 | tf_op jit(solution)/shard_map/while
  37.2 7.3 %copy-start = (f32[6,18,2050]{2,1,0:T(8,128)}, f32[6,18,2050]{2,1,0:T(8,128)S(1)}, u32[]{:S(2)}) copy-start(f32[6,18,2050]{2,1,0:T(8,128)S(1)} %get-tuple-element.307) | copy-start | bytes 2656804 | tf_op jit(solution)/shard_map/while
  49.1 2.5 %copy-start.2 = (f32[32768]{0:T(1024)S(1)}, f32[32768]{0:T(1024)}, u32[]{:S(2)}) copy-start(f32[32768]{0:T(1024)} %get-tuple-element.290) | copy-start | bytes 393220 | tf_op jit(solution)/shard_map/while
  51.6 1.3 %copy-start.1 = (f32[6,18,2050]{2,1,0:T(8,128)S(1)}, f32[6,18,2050]{2,1,0:T(8,128)}, u32[]{:S(2)}) copy-start(f32[6,18,2050]{2,1,0:T(8,128)} %copy-done) | copy-start | bytes 2656804 | tf_op jit(solution)/shard_map/while
  51.6 1.3 %copy-start.6 = (s32[4]{0:T(128)S(1)}, s32[4]{0:T(128)}, u32[]{:S(2)}) copy-start(s32[4]{0:T(128)} %copy-done.5) | copy-start | bytes 52 | tf_op jit(solution)/shard_map/while
  51.7 0.7 copy-start.3
  52.9 6.7 %copy-start.5 = (s32[4]{0:T(128)}, s32[4]{0:T(128)S(1)}, u32[]{:S(2)}) copy-start(s32[4]{0:T(128)S(1)} %get-tuple-element.306) | copy-start | bytes 52 | tf_op jit(solution)/shard_map/while
  52.9 7.3 %copy-start = (f32[6,18,2050]{2,1,0:T(8,128)}, f32[6,18,2050]{2,1,0:T(8,128)S(1)}, u32[]{:S(2)}) copy-start(f32[6,18,2050]{2,1,0:T(8,128)S(1)} %get-tuple-element.307) | copy-start | bytes 2656804 | tf_op jit(solution)/shard_map/while
  64.9 2.5 %copy-start.2 = (f32[32768]{0:T(1024)S(1)}, f32[32768]{0:T(1024)}, u32[]{:S(2)}) copy-start(f32[32768]{0:T(1024)} %get-tuple-element.290) | copy-start | bytes 393220 | tf_op jit(solution)/shard_map/while
  67.3 1.3 %copy-start.1 = (f32[6,18,2050]{2,1,0:T(8,128)S(1)}, f32[6,18,2050]{2,1,0:T(8,128)}, u32[]{:S(2)}) copy-start(f32[6,18,2050]{2,1,0:T(8,128)} %copy-done) | copy-start | bytes 2656804 | tf_op jit(solution)/shard_map/while
  67.3 1.3 %copy-start.6 = (s32[4]{0:T(128)S(1)}, s32[4]{0:T(128)}, u32[]{:S(2)}) copy-start(s32[4]{0:T(128)} %copy-done.5) | copy-start | bytes 52 | tf_op jit(solution)/shard_map/while
  67.4 0.7 copy-start.3
  68.7 6.7 %copy-start.5 = (s32[4]{0:T(128)}, s32[4]{0:T(128)S(1)}, u32[]{:S(2)}) copy-start(s32[4]{0:T(128)S(1)} %get-tuple-element.306) | copy-start | bytes 52 | tf_op jit(solution)/shard_map/while
  68.7 7.3 %copy-start = (f32[6,18,2050]{2,1,0:T(8,128)}, f32[6,18,2050]{2,1,0:T(8,128)S(1)}, u32[]{:S(2)}) copy-start(f32[6,18,2050]{2,1,0:T(8,128)S(1)} %get-tuple-element.307) | copy-start | bytes 2656804 | tf_op jit(solution)/shard_map/while
  80.6 2.5 %copy-start.2 = (f32[32768]{0:T(1024)S(1)}, f32[32768]{0:T(1024)}, u32[]{:S(2)}) copy-start(f32[32768]{0:T(1024)} %get-tuple-element.290) | copy-start | bytes 393220 | tf_op jit(solution)/shard_map/while
  83.1 1.3 %copy-start.1 = (f32[6,18,2050]{2,1,0:T(8,128)S(1)}, f32[6,18,2050]{2,1,0:T(8,128)}, u32[]{:S(2)}) copy-start(f32[6,18,2050]{2,1,0:T(8,128)} %copy-done) | copy-start | bytes 2656804 | tf_op jit(solution)/shard_map/while
  83.1 1.3 %copy-start.6 = (s32[4]{0:T(128)S(1)}, s32[4]{0:T(128)}, u32[]{:S(2)}) copy-start(s32[4]{0:T(128)} %copy-done.5) | copy-start | bytes 52 | tf_op jit(solution)/shard_map/while
  83.2 0.7 copy-start.3
where the time goes:
time: 131 us; the launch traced here: 130 us
  local copies, waits for them, and re-layouts  40.5 us (31%)
  blocking collectives  23 us (18%)
  loops' own time  20.8 us (16%)
  other arithmetic  19.3 us (15%)
  starting transfers between devices  12.4 us (9%)
  matrix products  8.57 us (7%)
  waiting for transfers between devices  4.66 us (4%)
    all_to_all x1, blocking collectives, on_device(): lax.all_to_all(partial_value, 'depth', split_axis=2, concat_axis=1, tiled...  23 us
    another operation x1, loops' own time, on_device(): lax.scan(advance, start, jnp.arange(slab_depth, dtype=jnp.int32))  20.8 us
    unnamed x8, local copies, waits for them, and re-layouts  11.1 us
    reduce_sum x4, other arithmetic, shade_slice(): jnp.sum(looked[:3 * material_count].reshape(material_count, 3, -1) * oneh...  9.79 us
    dot_general x4, matrix products, shade_slice(): jnp.dot(knot_table, tent_weights, precision=lax.Precision.HIGHEST, prefer...  8.57 us
    reshape x4, local copies, waits for them, and re-layouts, shade_slice(): looked[:3 * material_count].reshape(material_count, 3, -1)  8.23 us
    ppermute x2, starting transfers between devices, with_halo(): before = lax.ppermute(last, axis, up)  7.86 us
    while x72, local copies, waits for them, and re-layouts  7.4 us
  transfers between devices with their start and end apart: 4, of which 2 were waited for; matrix products, arithmetic and copies ran while one was open for 2% of the time, Pallas kernels for 0%

commit v1 on v0

--- a/solution.py
+++ b/solution.py
@@ -96,7 +96,12 @@
     groups = lax.axis_size("depth")
     levels = groups.bit_length() - 1
     block_width = columns // groups
-    pieces = lax.all_to_all(partial_value, "depth", split_axis=2, concat_axis=1, tiled=True)
+    pieces = jnp.concatenate(
+        lax.all_to_all(
+            jnp.stack(jnp.split(partial_value, lax.axis_size("depth"), axis=2)), "depth", 0, 0
+        ),
+        axis=1,
+    )
     pieces = pieces.reshape(4, groups, row_count, block_width)
     for section_bit in range(levels):
         pieces = composite_over(pieces[:, 0::2], pieces[:, 1::2])

time: 131 us -> 121 us (0.924)
  local copies, waits for them, and re-layouts: 40.5 us -> 29 us
  loops' own time: 20.8 us -> 22.8 us
    unnamed x8 -> x39, local copies, waits for them, and re-layouts: 11.1 us -> 4.31 us
    all_to_all x2 -> x1, local copies, waits for them, and re-layouts: 4.06 us -> 0.51 us  [on_device(): lax.all_to_all(jnp.stack(jnp.split(partial_value, lax.axis_size('depth'),...]
    concatenate x2, local copies, waits for them, and re-layouts: 4 us -> 0.94 us  [on_device(): jnp.concatenate([radiance, transmit[None, :]], axis=0)]
    dynamic_slice x4, local copies, waits for them, and re-layouts: 2.69 us -> 5.29 us  [on_device(): lax.scan(advance, start, jnp.arange(slab_depth, dtype=jnp.int32))]
    another operation x1, loops' own time: 20.8 us -> 22.8 us  [on_device(): lax.scan(advance, start, jnp.arange(slab_depth, dtype=jnp.int32))]
    slice x8 -> x4, local copies, waits for them, and re-layouts: 1.65 us -> 0.16 us  [on_device(): pieces = composite_over(pieces[:, 0::2], pieces[:, 1::2])]
    while x72 -> x56, local copies, waits for them, and re-layouts: 7.4 us -> 7.41 us
where the time goes in v1:
time: 121 us; the launch traced here: 120 us
  local copies, waits for them, and re-layouts  29 us (24%)
  blocking collectives  23 us (19%)
  loops' own time  22.8 us (19%)
  other arithmetic  19.2 us (16%)
  starting transfers between devices  12.4 us (10%)
  matrix products  8.57 us (7%)
  waiting for transfers between devices  4.66 us (4%)
    all_to_all x1, blocking collectives, on_device(): lax.all_to_all(jnp.stack(jnp.split(partial_value, lax.axis_size('depth'),...  23 us
    another operation x1, loops' own time, on_device(): lax.scan(advance, start, jnp.arange(slab_depth, dtype=jnp.int32))  22.8 us
    reduce_sum x4, other arithmetic, shade_slice(): jnp.sum(looked[:3 * material_count].reshape(material_count, 3, -1) * oneh...  9.79 us
    dot_general x4, matrix products, shade_slice(): jnp.dot(knot_table, tent_weights, precision=lax.Precision.HIGHEST, prefer...  8.57 us
    reshape x4, local copies, waits for them, and re-layouts, shade_slice(): looked[:3 * material_count].reshape(material_count, 3, -1)  8.26 us
    ppermute x2, starting transfers between devices, with_halo(): before = lax.ppermute(last, axis, up)  7.86 us
    while x56, local copies, waits for them, and re-layouts  7.41 us
    dynamic_slice x4, local copies, waits for them, and re-layouts, on_device(): lax.scan(advance, start, jnp.arange(slab_depth, dtype=jnp.int32))  5.29 us
  transfers between devices with their start and end apart: 4, of which 2 were waited for; matrix products, arithmetic and copies ran while one was open for 2% of the time, Pallas kernels for 0%

profile of v1, /device:TPU:225, one launch (start us, length us, event | category | flops | bytes accessed | tf_op | source)
XLA Modules:
  0.0 119.9 jit_solution(16835143069599641008)
XLA Ops:
  0.0 1.0 fusion.30
  1.0 2.6 %collective-permute-start.1 = (f32[1,16,2048]{2,1,0:T(8,128)S(1)}, f32[1,16,2048]{2,1,0:T(8,128)S(1)}, u32[]{:S(2)}, u32[]{:S(2)}) collective-permute-start(f32[1,16,2048]{2,1,0:T(8,128)S(1)} %get-tuple-element.202), channel_id=1, source_target_pairs={{16,0},{32,16},{48,32},{64,48},{80,64},{96,80},{112,96},{128,112},... | collective-permute-start | bytes 393224 | tf_op jit(solution)/shard_map/ppermute | solution.py:21
  3.6 3.1 %collective-permute-start = (f32[1,16,2048]{2,1,0:T(8,128)S(1)}, f32[1,16,2048]{2,1,0:T(8,128)S(1)}, u32[]{:S(2)}, u32[]{:S(2)}) collective-permute-start(f32[1,16,2048]{2,1,0:T(8,128)S(1)} %get-tuple-element.203), channel_id=1, source_target_pairs={{0,16},{16,32},{32,48},{48,64},{64,80},{80,96},{96,112},{112,128},... | collective-permute-start | bytes 393224 | tf_op jit(solution)/shard_map/ppermute | solution.py:20
  7.4 0.7 copy.70
  8.6 1.1 constant_dynamic-update-slice_fusion.1
  9.8 4.8 %collective-permute-start.2 = (f32[6,1,2048]{2,1,0:T(1,128)S(1)}, f32[6,1,2048]{2,1,0:T(1,128)S(1)}, u32[]{:S(2)}, u32[]{:S(2)}) collective-permute-start(f32[6,1,2048]{2,1,0:T(1,128)S(1)} %get-tuple-element.196), channel_id=1, source_target_pairs={{0,1},{1,2},{2,3},{3,4},{4,5},{5,6},{6,7},{7,8},{8,9},{9,10},{10,1... | collective-permute-start | bytes 147464 | tf_op jit(solution)/shard_map/ppermute | solution.py:20
  14.6 1.9 %collective-permute-start.3 = (f32[6,1,2048]{2,1,0:T(1,128)S(1)}, f32[6,1,2048]{2,1,0:T(1,128)S(1)}, u32[]{:S(2)}, u32[]{:S(2)}) collective-permute-start(f32[6,1,2048]{2,1,0:T(1,128)S(1)} %get-tuple-element.197), channel_id=1, source_target_pairs={{1,0},{2,1},{3,2},{4,3},{5,4},{6,5},{7,6},{8,7},{9,8},{10,9},{11,1... | collective-permute-start | bytes 147464 | tf_op jit(solution)/shard_map/ppermute | solution.py:21
  16.6 4.2 %collective-permute-done.3 = f32[6,1,2048]{2,1,0:T(1,128)S(1)} collective-permute-done((f32[6,1,2048]{2,1,0:T(1,128)S(1)}, f32[6,1,2048]{2,1,0:T(1,128)S(1)}, u32[]{:S(2)}, u32[]{:S(2)}) %collective-permute-start.3) | collective-permute-done | bytes 49184 | tf_op jit(solution)/shard_map/ppermute | solution.py:21
  22.0 67.7 %while.16 = (s32[]{:T(128)}, f32[3,32768]{1,0:T(4,128)S(1)}, f32[32768]{0:T(1024)}, s32[4]{0:T(128)}, f32[6,18,2050]{2,1,0:T(8,128)S(1)}, /*index=5*/f32[16,16]{...) while((s32[]{:T(128)}, f32[3,32768]{1,0:T(4,128)S(1)}, ...), condition=%wide.region_3.4_spmd.clone, body=%wide.region_0.3_spmd.clone.sunk | while | flops 105480208 | bytes 23315492 | solution.py:92
  22.0 1.3 %dynamic_slice.52 = s32[1]{0:T(128)} dynamic-slice(s32[4]{0:T(128)} %get-tuple-element.314, s32[]{:T(128)S(6)} %copy.90), dynamic_slice_sizes={1} | dynamic-slice | bytes 12 | tf_op jit(solution)/shard_map/while/body/jit(dynamic_index_in_dim)/dynamic_slice | solution.py:92
  28.9 0.9 dynamic-slice_bitcast_fusion.7
  30.4 2.1 %convolution_bitcast_fusion.2 = f32[16,32768]{1,0:T(8,128)S(1)} fusion(f32[16,16]{1,0:T(8,128)S(1)} %get-tuple-element.316, f32[32768]{0:T(1024)S(1)} %bitcast.203), kind=kOutput, calls=%fused_computation.1.clone.1 | convolution fusion | flops 102760448 | bytes 2229248 | tf_op jit(solution)/shard_map/while/body/eval_jaxpr/dot_general | solution.py:38
  33.0 2.1 %reshape.154 = f32[4,3,32768]{2,1,0:T(4,128)} reshape(f32[12,32768]{1,0:T(8,128)S(1)} %bitcast.197) | data formatting | bytes 3145728 | tf_op jit(solution)/shard_map/while/body/eval_jaxpr/reshape | solution.py:48
  35.1 2.4 %multiply_reduce_fusion.2 = f32[3,32768]{1,0:T(4,128)S(1)} fusion(f32[4,3,32768]{2,1,0:T(4,128)} %reshape.154, f32[4,32768]{1,0:T(4,128)S(1)} %fusion.40), kind=kLoop, calls=%fused_computation.2.clone.1 | loop fusion | flops 688128 | bytes 2490368 | tf_op jit(solution)/shard_map/while/body/eval_jaxpr/reduce_sum | solution.py:47
  38.9 1.3 %dynamic_slice.52 = s32[1]{0:T(128)} dynamic-slice(s32[4]{0:T(128)} %get-tuple-element.314, s32[]{:T(128)S(6)} %copy.90), dynamic_slice_sizes={1} | dynamic-slice | bytes 12 | tf_op jit(solution)/shard_map/while/body/jit(dynamic_index_in_dim)/dynamic_slice | solution.py:92
  45.8 0.9 dynamic-slice_bitcast_fusion.7
  47.4 2.1 %convolution_bitcast_fusion.2 = f32[16,32768]{1,0:T(8,128)S(1)} fusion(f32[16,16]{1,0:T(8,128)S(1)} %get-tuple-element.316, f32[32768]{0:T(1024)S(1)} %bitcast.203), kind=kOutput, calls=%fused_computation.1.clone.1 | convolution fusion | flops 102760448 | bytes 2229248 | tf_op jit(solution)/shard_map/while/body/eval_jaxpr/dot_general | solution.py:38
  50.0 2.1 %reshape.154 = f32[4,3,32768]{2,1,0:T(4,128)} reshape(f32[12,32768]{1,0:T(8,128)S(1)} %bitcast.197) | data formatting | bytes 3145728 | tf_op jit(solution)/shard_map/while/body/eval_jaxpr/reshape | solution.py:48
  52.0 2.4 %multiply_reduce_fusion.2 = f32[3,32768]{1,0:T(4,128)S(1)} fusion(f32[4,3,32768]{2,1,0:T(4,128)} %reshape.154, f32[4,32768]{1,0:T(4,128)S(1)} %fusion.40), kind=kLoop, calls=%fused_computation.2.clone.1 | loop fusion | flops 688128 | bytes 2490368 | tf_op jit(solution)/shard_map/while/body/eval_jaxpr/reduce_sum | solution.py:47
  55.8 1.3 %dynamic_slice.52 = s32[1]{0:T(128)} dynamic-slice(s32[4]{0:T(128)} %get-tuple-element.314, s32[]{:T(128)S(6)} %copy.90), dynamic_slice_sizes={1} | dynamic-slice | bytes 12 | tf_op jit(solution)/shard_map/while/body/jit(dynamic_index_in_dim)/dynamic_slice | solution.py:92
  62.7 0.9 dynamic-slice_bitcast_fusion.7
  64.3 2.1 %convolution_bitcast_fusion.2 = f32[16,32768]{1,0:T(8,128)S(1)} fusion(f32[16,16]{1,0:T(8,128)S(1)} %get-tuple-element.316, f32[32768]{0:T(1024)S(1)} %bitcast.203), kind=kOutput, calls=%fused_computation.1.clone.1 | convolution fusion | flops 102760448 | bytes 2229248 | tf_op jit(solution)/shard_map/while/body/eval_jaxpr/dot_general | solution.py:38
  66.9 2.1 %reshape.154 = f32[4,3,32768]{2,1,0:T(4,128)} reshape(f32[12,32768]{1,0:T(8,128)S(1)} %bitcast.197) | data formatting | bytes 3145728 | tf_op jit(solution)/shard_map/while/body/eval_jaxpr/reshape | solution.py:48
  69.0 2.4 %multiply_reduce_fusion.2 = f32[3,32768]{1,0:T(4,128)S(1)} fusion(f32[4,3,32768]{2,1,0:T(4,128)} %reshape.154, f32[4,32768]{1,0:T(4,128)S(1)} %fusion.40), kind=kLoop, calls=%fused_computation.2.clone.1 | loop fusion | flops 688128 | bytes 2490368 | tf_op jit(solution)/shard_map/while/body/eval_jaxpr/reduce_sum | solution.py:47
  72.8 1.3 %dynamic_slice.52 = s32[1]{0:T(128)} dynamic-slice(s32[4]{0:T(128)} %get-tuple-element.314, s32[]{:T(128)S(6)} %copy.90), dynamic_slice_sizes={1} | dynamic-slice | bytes 12 | tf_op jit(solution)/shard_map/while/body/jit(dynamic_index_in_dim)/dynamic_slice | solution.py:92
  79.7 0.9 dynamic-slice_bitcast_fusion.7
  81.2 2.1 %convolution_bitcast_fusion.2 = f32[16,32768]{1,0:T(8,128)S(1)} fusion(f32[16,16]{1,0:T(8,128)S(1)} %get-tuple-element.316, f32[32768]{0:T(1024)S(1)} %bitcast.203), kind=kOutput, calls=%fused_computation.1.clone.1 | convolution fusion | flops 102760448 | bytes 2229248 | tf_op jit(solution)/shard_map/while/body/eval_jaxpr/dot_general | solution.py:38
  83.8 2.1 %reshape.154 = f32[4,3,32768]{2,1,0:T(4,128)} reshape(f32[12,32768]{1,0:T(8,128)S(1)} %bitcast.197) | data formatting | bytes 3145728 | tf_op jit(solution)/shard_map/while/body/eval_jaxpr/reshape | solution.py:48
  85.9 2.4 %multiply_reduce_fusion.2 = f32[3,32768]{1,0:T(4,128)S(1)} fusion(f32[4,3,32768]{2,1,0:T(4,128)} %reshape.154, f32[4,32768]{1,0:T(4,128)S(1)} %fusion.40), kind=kLoop, calls=%fused_computation.2.clone.1 | loop fusion | flops 688128 | bytes 2490368 | tf_op jit(solution)/shard_map/while/body/eval_jaxpr/reduce_sum | solution.py:47
  89.7 0.9 concatenate.35
  92.9 23.0 %all_to_all.5 = f32[32,1,4096]{2,1,0:T(1,128)S(1)} all-to-all(f32[32,1,4096]{2,1,0:T(1,128)S(1)} %reshape.151), channel_id=1, replica_groups=mesh['depth'=32,'strip'=16] {'depth'}, dimensions={0} | all-to-all | bytes 1048576 | tf_op jit(solution)/shard_map/all_to_all | solution.py:100
  116.4 1.9 %reduce = f32[32,4096]{1,0:T(8,128)S(1)} reduce(f32[32,1,4096]{2,1,0:T(1,128)S(1)} %all_to_all.5, f32[]{:T(128)} %broadcast.229), dimensions={1}, to_apply=%all_to_all.3.reduce_sub_computation | reduce | bytes 1048580 | tf_op jit(solution)/shard_map/all_to_all | solution.py:100
  (147 shorter events, 16.0 us)
Async XLA Ops:
  0.0 16.5 %copy-start.4 = (f32[4,16]{1,0:T(4,128)S(1)}, f32[4,16]{1,0:T(4,128)}, u32[]{:S(2)}) copy-start(f32[4,16]{1,0:T(4,128)} %param.11) | copy-start | bytes 772
  1.0 8.7 %collective-permute-start.1 = (f32[1,16,2048]{2,1,0:T(8,128)S(1)}, f32[1,16,2048]{2,1,0:T(8,128)S(1)}, u32[]{:S(2)}, u32[]{:S(2)}) collective-permute-start(f32[1,16,2048]{2,1,0:T(8,128)S(1)} %get-tuple-element.202), channel_id=1, source_target_pairs={{16,0},{32,16},{48,32},{64,48},{80,64},{96,80},{112,96},{128,112},... | collective-permute-start | bytes 393224 | tf_op jit(solution)/shard_map/ppermute | solution.py:21
  3.6 5.0 %collective-permute-start = (f32[1,16,2048]{2,1,0:T(8,128)S(1)}, f32[1,16,2048]{2,1,0:T(8,128)S(1)}, u32[]{:S(2)}, u32[]{:S(2)}) collective-permute-start(f32[1,16,2048]{2,1,0:T(8,128)S(1)} %get-tuple-element.203), channel_id=1, source_target_pairs={{0,16},{16,32},{32,48},{48,64},{64,80},{80,96},{96,112},{112,128},... | collective-permute-start | bytes 393224 | tf_op jit(solution)/shard_map/ppermute | solution.py:20
  9.8 6.7 %collective-permute-start.2 = (f32[6,1,2048]{2,1,0:T(1,128)S(1)}, f32[6,1,2048]{2,1,0:T(1,128)S(1)}, u32[]{:S(2)}, u32[]{:S(2)}) collective-permute-start(f32[6,1,2048]{2,1,0:T(1,128)S(1)} %get-tuple-element.196), channel_id=1, source_target_pairs={{0,1},{1,2},{2,3},{3,4},{4,5},{5,6},{6,7},{7,8},{8,9},{9,10},{10,1... | collective-permute-start | bytes 147464 | tf_op jit(solution)/shard_map/ppermute | solution.py:20
  14.6 6.1 %collective-permute-start.3 = (f32[6,1,2048]{2,1,0:T(1,128)S(1)}, f32[6,1,2048]{2,1,0:T(1,128)S(1)}, u32[]{:S(2)}, u32[]{:S(2)}) collective-permute-start(f32[6,1,2048]{2,1,0:T(1,128)S(1)} %get-tuple-element.197), channel_id=1, source_target_pairs={{1,0},{2,1},{3,2},{4,3},{5,4},{6,5},{7,6},{8,7},{9,8},{10,9},{11,1... | collective-permute-start | bytes 147464 | tf_op jit(solution)/shard_map/ppermute | solution.py:21
  22.0 8.4 %copy-start = (f32[6,18,2050]{2,1,0:T(8,128)}, f32[6,18,2050]{2,1,0:T(8,128)S(1)}, u32[]{:S(2)}) copy-start(f32[6,18,2050]{2,1,0:T(8,128)S(1)} %get-tuple-element.315) | copy-start | bytes 2656804 | tf_op jit(solution)/shard_map/while
  35.1 2.5 %copy-start.2 = (f32[32768]{0:T(1024)S(1)}, f32[32768]{0:T(1024)}, u32[]{:S(2)}) copy-start(f32[32768]{0:T(1024)} %get-tuple-element.298) | copy-start | bytes 393220 | tf_op jit(solution)/shard_map/while
  37.5 1.3 %copy-start.1 = (f32[6,18,2050]{2,1,0:T(8,128)S(1)}, f32[6,18,2050]{2,1,0:T(8,128)}, u32[]{:S(2)}) copy-start(f32[6,18,2050]{2,1,0:T(8,128)} %copy-done) | copy-start | bytes 2656804 | tf_op jit(solution)/shard_map/while
  37.6 0.6 copy-start.3
  38.9 8.4 %copy-start = (f32[6,18,2050]{2,1,0:T(8,128)}, f32[6,18,2050]{2,1,0:T(8,128)S(1)}, u32[]{:S(2)}) copy-start(f32[6,18,2050]{2,1,0:T(8,128)S(1)} %get-tuple-element.315) | copy-start | bytes 2656804 | tf_op jit(solution)/shard_map/while
  52.0 2.5 %copy-start.2 = (f32[32768]{0:T(1024)S(1)}, f32[32768]{0:T(1024)}, u32[]{:S(2)}) copy-start(f32[32768]{0:T(1024)} %get-tuple-element.298) | copy-start | bytes 393220 | tf_op jit(solution)/shard_map/while
  54.5 1.3 %copy-start.1 = (f32[6,18,2050]{2,1,0:T(8,128)S(1)}, f32[6,18,2050]{2,1,0:T(8,128)}, u32[]{:S(2)}) copy-start(f32[6,18,2050]{2,1,0:T(8,128)} %copy-done) | copy-start | bytes 2656804 | tf_op jit(solution)/shard_map/while
  54.6 0.6 copy-start.3
  55.8 8.4 %copy-start = (f32[6,18,2050]{2,1,0:T(8,128)}, f32[6,18,2050]{2,1,0:T(8,128)S(1)}, u32[]{:S(2)}) copy-start(f32[6,18,2050]{2,1,0:T(8,128)S(1)} %get-tuple-element.315) | copy-start | bytes 2656804 | tf_op jit(solution)/shard_map/while
  69.0 2.5 %copy-start.2 = (f32[32768]{0:T(1024)S(1)}, f32[32768]{0:T(1024)}, u32[]{:S(2)}) copy-start(f32[32768]{0:T(1024)} %get-tuple-element.298) | copy-start | bytes 393220 | tf_op jit(solution)/shard_map/while
  71.4 1.3 %copy-start.1 = (f32[6,18,2050]{2,1,0:T(8,128)S(1)}, f32[6,18,2050]{2,1,0:T(8,128)}, u32[]{:S(2)}) copy-start(f32[6,18,2050]{2,1,0:T(8,128)} %copy-done) | copy-start | bytes 2656804 | tf_op jit(solution)/shard_map/while
  71.5 0.6 copy-start.3
  72.8 8.4 %copy-start = (f32[6,18,2050]{2,1,0:T(8,128)}, f32[6,18,2050]{2,1,0:T(8,128)S(1)}, u32[]{:S(2)}) copy-start(f32[6,18,2050]{2,1,0:T(8,128)S(1)} %get-tuple-element.315) | copy-start | bytes 2656804 | tf_op jit(solution)/shard_map/while
  85.9 2.5 %copy-start.2 = (f32[32768]{0:T(1024)S(1)}, f32[32768]{0:T(1024)}, u32[]{:S(2)}) copy-start(f32[32768]{0:T(1024)} %get-tuple-element.298) | copy-start | bytes 393220 | tf_op jit(solution)/shard_map/while
  88.4 1.3 %copy-start.1 = (f32[6,18,2050]{2,1,0:T(8,128)S(1)}, f32[6,18,2050]{2,1,0:T(8,128)}, u32[]{:S(2)}) copy-start(f32[6,18,2050]{2,1,0:T(8,128)} %copy-done) | copy-start | bytes 2656804 | tf_op jit(solution)/shard_map/while
  88.4 0.6 copy-start.3
